TPU v7x, 256 devices: a whole 4x4x8 slice. The times are simulated.
256 devices in a mesh: tm: 8 (over x, core), row: 32 (over z, y).
Axes of the slice: x: 4, y: 4, z: 8, core: 2. Of those that a mesh axis runs over, the one named last changes fastest.
Arguments:
- pred_cov: bfloat16 [8, 1536, 1536], P('tm', 'row'), may hold values from -0.8 to 3.3, as said below
- cross: float32 [8, 1536, 1536], P('tm', 'row'), may hold values from -0.9 to 3.2
- filt_mean: float32 [8, 1536], P('tm', 'row'), may hold values from -6 to 6
- pred_mean: float32 [8, 1536], P('tm', 'row'), may hold values from -6 to 6
- next_smoothed: float32 [1536], P('row'), may hold values from -6 to 6
Outputs:
- smoothed: float32 [8, 1536], P('tm', 'row')
- gains: float32 [8, 1536, 1536], P('tm', 'row')
Inputs may be any that keep to these rules, and one draw needn't show every extreme that they name: `pred_cov`: each of the 8 matrices of size 1536 x 1536 is symmetric positive definite.
All inputs are finite; a program needn't handle non-finite values.
Results may differ from a plain program's by a relative error of at most 0.0003.
Values may be sent and summed in bfloat16 or wider, within the bound.
No kernel may reach another device: no remote copies, remote signals or barrier semaphores. Data moves between devices by JAX's collectives and lax.ppermute only.
A program may use at most 128 MiB of HBM per device.

v0:
```python
import functools

import jax
import jax.numpy as jnp
from jax import lax
from jax.experimental import pallas as pl
from jax.experimental.pallas import tpu as pltpu
from jax.sharding import PartitionSpec as P

f32, bf16 = jnp.float32, jnp.bfloat16
N, LANES = 1536, 128
MINE = 48
PIECE = 4 * MINE
B = 2 * PIECE
H = 128
TILE = 512
Y, Z = 4, 8
VMEM_WHOLE = pl.BlockSpec(memory_space=pltpu.VMEM)
SMEM_WHOLE = pl.BlockSpec(memory_space=pltpu.SMEM)

def inv4(d):
    a,b,c=d[0][0],d[1][0],d[1][1]
    r=1.0/(a*c-b*b)
    p,q,s=c*r,-b*r,a*r
    e0,e1,g0,g1=d[2][0],d[2][1],d[3][0],d[3][1]
    x00,x01=e0*p+e1*q,e0*q+e1*s
    x10,x11=g0*p+g1*q,g0*q+g1*s
    u=d[2][2]-(x00*e0+x01*e1)
    v=d[3][2]-(x10*e0+x11*e1)
    w=d[3][3]-(x10*g0+x11*g1)
    r2=1.0/(u*w-v*v)
    U,V,W=w*r2,-v*r2,u*r2
    y00,y01=U*x00+V*x10,U*x01+V*x11
    y10,y11=V*x00+W*x10,V*x01+W*x11
    i00=p+x00*y00+x10*y10
    i01=q+x00*y01+x10*y11
    i11=s+x01*y01+x11*y11
    return [[i00,i01,-y00,-y10],[i01,i11,-y01,-y11],[-y00,-y01,U,V],[-y10,-y11,V,W]]

def leaf(m_ref, K=4):
    n=m_ref.shape[0]
    lane=lax.broadcasted_iota(jnp.int32,(1,n),1)
    lanef=lax.broadcasted_iota(jnp.int32,(n,n),1)
    for p0 in range(0,n,K):
        M=m_ref[...]
        c=[jnp.broadcast_to(M[:,p0+q:p0+q+1],(n,n)) for q in range(K)]
        d=[[c[j][p0+i:p0+i+1,:] for j in range(i+1)] for i in range(K)]
        Di=inv4(d)
        r=[M[p0+q:p0+q+1,:] for q in range(K)]
        t=[]
        for i in range(K):
            x=Di[i][0]*r[0]
            for j in range(1,K): x=x+Di[i][j]*r[j]
            for j in range(K): x=jnp.where(lane==p0+j,-Di[i][j],x)
            t.append(x)
        new=jnp.where((lanef>=p0)&(lanef<p0+K),0.0,M)
        for q in range(K): new=new-c[q]*t[q]
        m_ref[...]=new
        m_ref[p0:p0+K,:]=jnp.concatenate(t,0)


def split(x):
    h = x.astype(bf16)
    return h, (x - h.astype(f32)).astype(bf16)


def wide(x):
    h, l = split(x)
    return jnp.concatenate([h, h, l], 1)


def tall(x):
    h, l = split(x)
    return jnp.concatenate([h, l, h], 0)


def dot(a, b):
    return jnp.dot(a, b, preferred_element_type=f32)


def block_sweep(d_ref, m_ref, r_ref):
    def step(k, _):
        o = pl.multiple_of(k * H, H)
        m_ref[...] = d_ref[pl.ds(o, H), pl.ds(o, H)]
        leaf(m_ref)
        minus = m_ref[...]
        t = -dot(wide(minus), tall(d_ref[pl.ds(o, H), :]))
        c = wide(d_ref[:, pl.ds(o, H)])
        r_ref[...] = -dot(c, tall(minus))
        d_ref[...] = d_ref[...] - dot(c, tall(t))
        d_ref[pl.ds(o, H), :] = t
        d_ref[:, pl.ds(o, H)] = r_ref[...]
        d_ref[pl.ds(o, H), pl.ds(o, H)] = minus
        return 0

    lax.fori_loop(0, B // H, step, 0)


def stage_kernel(stage, ids, block_ref, *refs):
    if stage:
        _, *refs = refs
    w_ref, p_ref, t3_ref, d_ref, m_ref, r_ref = refs
    here = pl.multiple_of(ids[stage] * B, B)
    for n in range(2):
        for d in range(Y):
            y = lax.rem(ids[6] + d, Y)
            to = pl.multiple_of(lax.rem(ids[4 + n], 2) * PIECE + y * MINE, 16)
            at = (2 * d + n) * MINE
            p_ref[pl.ds(to, MINE), :] = block_ref[at : at + MINE, :]
    rows = pl.ds(here, B)
    w_ref[rows, :] = p_ref[...].astype(f32)
    if stage:

        def clear(j, _):
            w_ref[rows, pl.ds(pl.multiple_of(ids[j] * B, B), B)] = jnp.zeros((B, B), f32)
            return 0

        lax.fori_loop(0, stage, clear, 0)

        def earlier(j, _):
            there = pl.multiple_of(ids[j] * B, B)
            p = p_ref[:, pl.ds(there, B)]
            p = jnp.concatenate([p, p], 1)

            def tile(n, _):
                q = pl.ds(pl.multiple_of(n * TILE, TILE), TILE)
                h, l = split(w_ref[pl.ds(there, B), q])
                w_ref[rows, q] = w_ref[rows, q] - dot(p, jnp.concatenate([h, l], 0))
                return 0

            return lax.fori_loop(0, N // TILE, tile, 0)

        lax.fori_loop(0, stage, earlier, 0)
    d_ref[...] = w_ref[rows, pl.ds(here, B)]
    block_sweep(d_ref, m_ref, r_ref)
    minus = d_ref[...]
    left = wide(minus)

    def forward(n, _):
        q = pl.ds(pl.multiple_of(n * TILE, TILE), TILE)
        t = -dot(left, tall(w_ref[rows, q]))
        t3_ref[:, q] = tall(t)
        w_ref[rows, q] = t
        return 0

    lax.fori_loop(0, N // TILE, forward, 0)
    w_ref[rows, pl.ds(here, B)] = minus
    if stage:

        def update(j, _):
            back = pl.ds(pl.multiple_of(ids[j] * B, B), B)
            c = wide(w_ref[back, pl.ds(here, B)])
            d_ref[...] = -dot(c, tall(minus))

            def tile(n, _):
                q = pl.ds(pl.multiple_of(n * TILE, TILE), TILE)
                w_ref[back, q] = w_ref[back, q] - dot(c, t3_ref[:, q])
                return 0

            lax.fori_loop(0, N // TILE, tile, 0)
            w_ref[back, pl.ds(here, B)] = d_ref[...]
            return 0

        lax.fori_loop(0, stage, update, 0)


def gain_kernel(cross_ref, w_ref, g_ref):
    c3 = wide(cross_ref[...])

    def gains(j, _):
        q = pl.ds(pl.multiple_of(j * B, B), B)
        g_ref[:, q] = -dot(c3, tall(w_ref[:, q]))
        return 0

    lax.fori_loop(0, N // B, gains, 0)


def gain_rows(cross, minus_inverse):
    return pl.pallas_call(
        gain_kernel,
        name="gains",
        out_shape=jax.ShapeDtypeStruct(cross.shape, f32),
        in_specs=[VMEM_WHOLE] * 2,
        out_specs=VMEM_WHOLE,
        compiler_params=pltpu.CompilerParams(vmem_limit_bytes=12 << 20),
        cost_estimate=pl.CostEstimate(flops=1_000_000_000, bytes_accessed=4 * N * N, transcendentals=0),
    )(cross, minus_inverse)


def sweep_stage(stage, ids, block, w):
    args = [ids, block] + ([w] if stage else [])
    return pl.pallas_call(
        functools.partial(stage_kernel, stage),
        name="stage" + str(stage),
        out_shape=jax.ShapeDtypeStruct((N, N), f32),
        in_specs=[SMEM_WHOLE] + [VMEM_WHOLE] * (len(args) - 1),
        out_specs=VMEM_WHOLE,
        scratch_shapes=[
            pltpu.VMEM((B, N), bf16),
            pltpu.VMEM((3 * B, N), bf16),
            pltpu.VMEM((B, B), f32),
            pltpu.VMEM((H, H), f32),
            pltpu.VMEM((B, H), f32),
        ],
        input_output_aliases={2: 0} if stage else {},
        compiler_params=pltpu.CompilerParams(vmem_limit_bytes=STAGE_VMEM),
        cost_estimate=pl.CostEstimate(flops=40_000_000_000, bytes_accessed=4 * B * N, transcendentals=0),
    )(*args)


STAGE_VMEM = 24 << 20


def matvec(m_ref, v_ref, out_ref, part_ref):
    def block(i, _):
        rows = pl.ds(pl.multiple_of(i * LANES, LANES), LANES)
        total = m_ref[rows, :LANES] * v_ref[:, :LANES]
        for j in range(1, N // LANES):
            lanes = slice(j * LANES, (j + 1) * LANES)
            total = total + m_ref[rows, lanes] * v_ref[:, lanes]
        part_ref[rows, :] = total
        return 0

    lax.fori_loop(0, N // LANES, block, 0)
    for i in range(N // LANES):
        rows = slice(i * LANES, (i + 1) * LANES)
        out_ref[:, rows] = jnp.sum(part_ref[rows, :].T, axis=0, keepdims=True)


def turn_kernel(n, mine_ref, *refs):
    if n:
        late_ref, before_ref, base_ref, mean_ref, w_ref, x_ref, s_ref, v_ref, y_ref, part_ref = refs
    else:
        w_ref, x_ref, s_ref, base_ref, mean_ref, v_ref, y_ref, part_ref = refs
        for j in range(N // LANES):
            rows = slice(j * LANES, (j + 1) * LANES)
            vectors = x_ref[rows, N:].T[:8, :]
            mean_ref[:, rows] = vectors[0:1]
            base_ref[:, rows] = jnp.where(mine_ref[0] == 0, vectors[2:3], 0.0) - vectors[1:2]

    @pl.when(mine_ref[0] == n)
    def _():
        v_ref[...] = late_ref[...] + base_ref[...] if n else base_ref[...]
        matvec(w_ref, v_ref, y_ref, part_ref)
        matvec(x_ref, y_ref, s_ref, part_ref)
        s_ref[...] = mean_ref[...] - s_ref[...]

    @pl.when(mine_ref[0] != n)
    def _():
        s_ref[...] = before_ref[...] if n else mean_ref[...]


def turn(n, mine, *args):
    return pl.pallas_call(
        functools.partial(turn_kernel, n),
        name="turn" + str(n),
        out_shape=[jax.ShapeDtypeStruct((1, N), f32)] * (1 if n else 3),
        in_specs=[SMEM_WHOLE] + [VMEM_WHOLE] * len(args),
        out_specs=[VMEM_WHOLE] * (1 if n else 3),
        scratch_shapes=[pltpu.VMEM((1, N), f32), pltpu.VMEM((1, N), f32), pltpu.VMEM((N, LANES), f32)],
        compiler_params=pltpu.CompilerParams(vmem_limit_bytes=4 << 20),
        cost_estimate=pl.CostEstimate(flops=4 * N * N, bytes_accessed=8 * N * N, transcendentals=0),
    )(mine, *args)


def swap(x, inner):
    pairs = []
    for z in range(Z):
        other = z ^ 1 if inner else (z + (1 if z % 2 else -1)) % Z
        pairs += [(z * Y + y, other * Y + y) for y in range(Y)]
    return lax.ppermute(x, "row", pairs)


def along_y(x, d):
    return lax.ppermute(x, "row", [(z * Y + (y + d) % Y, z * Y + y) for z in range(Z) for y in range(Y)])


def per_device(pred_cov, cross, filt_mean, pred_mean, next_smoothed):
    steps = lax.axis_size("tm")
    row = lax.axis_index("row")
    y, z = row % Y, row // Y
    columns = jnp.stack([filt_mean[0], pred_mean[0], next_smoothed], axis=1)
    packed = jnp.concatenate([cross[0], jnp.pad(columns, ((0, 0), (0, LANES - 3)))], axis=1)
    first = (row * MINE).astype(jnp.uint32)
    mine = (steps - 1 - lax.axis_index("tm")).astype(jnp.int32)[None]
    pred_cov, first, mine = lax.optimization_barrier((pred_cov, first, mine))

    pair = jnp.concatenate([pred_cov[0], swap(pred_cov[0], True)], axis=0)
    pairs = [pair] + [along_y(pair, d) for d in range(1, Y)]
    own = jnp.concatenate(pairs, axis=0)
    packed, own = lax.optimization_barrier((packed, own))
    packed = lax.all_gather(packed, "row", axis=0, tiled=True)
    block1 = swap(own, False)
    block2 = swap(block1, True)
    block3 = swap(block2, False)
    e = 1 - 2 * (z % 2)
    at = lambda k: (z + e * k + Z) % Z
    order = [at(0) // 2, at(-1) // 2, at(2) // 2, at(-3) // 2]
    ids = lambda m, n: jnp.stack(order + [at(m), at(n), y, y]).astype(jnp.int32)
    w = sweep_stage(0, ids(0, 1), own, None)
    w = sweep_stage(1, ids(-1, -2), block1, w)
    w = sweep_stage(2, ids(2, 3), block2, w)
    w = sweep_stage(3, ids(-3, -4), block3, w)

    state, base, mean = turn(0, mine, w, packed)
    for n in range(1, steps):
        late = lax.ppermute(state, "tm", [(steps - n, steps - n - 1)])
        if n == steps // 2:
            gain = gain_rows(cross[0], w)
            late, gain = lax.optimization_barrier((late, gain))
        (state,) = turn(n, mine, late, state, base, mean, w, packed)
    smoothed = lax.dynamic_slice(state[0], (first,), (MINE,))
    return (smoothed[None, :], gain[None, :, :])


def solution(mesh):
    in_specs = (
        P("tm", "row", None),
        P("tm", "row", None),
        P("tm", "row"),
        P("tm", "row"),
        P("row"),
    )
    out_specs = (P("tm", "row"), P("tm", "row", None))
    return jax.shard_map(
        per_device, mesh=mesh, in_specs=in_specs, out_specs=out_specs, check_vma=False
    )
```

profile of v0, /device:TPU:1, one launch (start us, length us, event | category | flops | bytes accessed | tf_op | source)
XLA Modules:
  0.0 264.5 jit_solution(1251682364747939846)
XLA Ops:
  7.2 2.6 collective-permute-start
  9.8 1.0 constant_dynamic-update-slice_fusion.4
  10.7 0.7 pad_maximum_fusion.1
  11.5 1.1 collective-permute-done
  12.6 0.9 pad_maximum_fusion
  13.5 3.7 %collective-permute-start.1 = (bf16[96,1536]{1,0:T(8,128)(2,1)S(1)}, bf16[96,1536]{1,0:T(8,128)(2,1)S(1)}, u32[]{:S(2)}, u32[]{:S(2)}) collective-permute-start(bf16[96,1536]{1,0:T(8,128)(2,1)S(1)} %pad_maximum_fusion), channel_id=1, source_target_pairs={{1,0},{2,1},{3,2},{0,3},{5,4},{6,5},{7,6},{4,7},{9,8},{10,9},{11,1... | collective-permute-start | bytes 884744 | tf_op jit(solution)/shard_map/ppermute | solution.py:275
  17.2 1.7 select_maximum_fusion
  19.2 0.7 collective-permute-start.3
  19.9 3.7 %collective-permute-done.1 = bf16[96,1536]{1,0:T(8,128)(2,1)S(1)} collective-permute-done((bf16[96,1536]{1,0:T(8,128)(2,1)S(1)}, bf16[96,1536]{1,0:T(8,128)(2,1)S(1)}, u32[]{:S(2)}, u32[]{:S(2)}) %collective-permute-start.1) | collective-permute-done | bytes 294944 | tf_op jit(solution)/shard_map/ppermute | solution.py:275
  23.6 3.7 %collective-permute-done.2 = bf16[96,1536]{1,0:T(8,128)(2,1)S(1)} collective-permute-done((bf16[96,1536]{1,0:T(8,128)(2,1)S(1)}, bf16[96,1536]{1,0:T(8,128)(2,1)S(1)}, u32[]{:S(2)}, u32[]{:S(2)}) %collective-permute-start.2) | collective-permute-done | bytes 294944 | tf_op jit(solution)/shard_map/ppermute | solution.py:275
  27.4 8.3 %collective-permute-done.3 = bf16[96,1536]{1,0:T(8,128)(2,1)S(1)} collective-permute-done((bf16[96,1536]{1,0:T(8,128)(2,1)S(1)}, bf16[96,1536]{1,0:T(8,128)(2,1)S(1)}, u32[]{:S(2)}, u32[]{:S(2)}) %collective-permute-start.3) | collective-permute-done | bytes 294944 | tf_op jit(solution)/shard_map/ppermute | solution.py:275
  36.3 5.2 %collective-permute-start.4 = (bf16[384,1536]{1,0:T(8,128)(2,1)S(1)}, bf16[384,1536]{1,0:T(8,128)(2,1)S(1)}, u32[]{:S(2)}, u32[]{:S(2)}) collective-permute-start(bf16[384,1536]{1,0:T(8,128)(2,1)S(1)} %constant_dynamic-update-slice_fusion.block_ref), channel_id=1, source_target_pairs={{0,28},{1,29},{2,30},{3,31},{4,8},{5,9},{6,10},{7,11},{8,4},{9,5},... | collective-permute-start | bytes 3538952 | tf_op jit(solution)/shard_map/ppermute | solution.py:271
  41.5 21.4 %stage0.1.refs_0_ = f32[1536,1536]{1,0:T(8,128)S(1)} custom-call(s32[8]{0:T(128)S(1)} %stack.94.ids, bf16[384,1536]{1,0:T(8,128)(2,1)S(1)} %constant_dynamic-update-slice_fusion.block_ref), custom_call_target="tpu_custom_call" | custom-call | flops 40000000000 | bytes 2359296 | tf_op jit(solution)/shard_map/stage0/pallas_call | solution.py:192
  63.0 16.1 %collective-permute-done.4.block_ref = bf16[384,1536]{1,0:T(8,128)(2,1)S(1)} collective-permute-done((bf16[384,1536]{1,0:T(8,128)(2,1)S(1)}, bf16[384,1536]{1,0:T(8,128)(2,1)S(1)}, u32[]{:S(2)}, u32[]{:S(2)}) %collective-permute-start.4) | collective-permute-done | bytes 1179680 | tf_op jit(solution)/shard_map/ppermute | solution.py:271
  79.1 25.7 %stage1.1.refs_0_ = f32[1536,1536]{1,0:T(8,128)S(1)} custom-call(s32[8]{0:T(128)S(1)} %stack.91.ids, bf16[384,1536]{1,0:T(8,128)(2,1)S(1)} %collective-permute-done.4.block_ref, f32[1536,1536]{1,0:T(8,128)S(1)} %stage0.1.refs_0_), custom_call_target="tpu_custom_call", output_to_operand_aliasing={{}: (2, {})} | custom-call | flops 40000000000 | bytes 2359296 | tf_op jit(solution)/shard_map/stage1/pallas_call | solution.py:192
  104.8 14.5 %collective-permute-done.5.block_ref = bf16[384,1536]{1,0:T(8,128)(2,1)S(1)} collective-permute-done((bf16[384,1536]{1,0:T(8,128)(2,1)S(1)}, bf16[384,1536]{1,0:T(8,128)(2,1)S(1)}, u32[]{:S(2)}, u32[]{:S(2)}) %collective-permute-start.5) | collective-permute-done | bytes 1179680 | tf_op jit(solution)/shard_map/ppermute | solution.py:271
  120.0 30.3 %stage2.1.refs_0_ = f32[1536,1536]{1,0:T(8,128)S(1)} custom-call(s32[8]{0:T(128)S(1)} %stack.88.ids, bf16[384,1536]{1,0:T(8,128)(2,1)S(1)} %collective-permute-done.5.block_ref, f32[1536,1536]{1,0:T(8,128)S(1)} %stage1.1.refs_0_), custom_call_target="tpu_custom_call", output_to_operand_aliasing={{}: (2, {})} | custom-call | flops 40000000000 | bytes 2359296 | tf_op jit(solution)/shard_map/stage2/pallas_call | solution.py:192
  150.3 21.2 %collective-permute-done.6.block_ref = bf16[384,1536]{1,0:T(8,128)(2,1)S(1)} collective-permute-done((bf16[384,1536]{1,0:T(8,128)(2,1)S(1)}, bf16[384,1536]{1,0:T(8,128)(2,1)S(1)}, u32[]{:S(2)}, u32[]{:S(2)}) %collective-permute-start.6) | collective-permute-done | bytes 1179680 | tf_op jit(solution)/shard_map/ppermute | solution.py:271
  171.5 34.6 %stage3.1.refs_0_.refs_4_.w_ref = f32[1536,1536]{1,0:T(8,128)S(1)} custom-call(s32[8]{0:T(128)S(1)} %stack.83.ids, bf16[384,1536]{1,0:T(8,128)(2,1)S(1)} %collective-permute-done.6.block_ref, f32[1536,1536]{1,0:T(8,128)S(1)} %stage2.1.refs_0_), custom_call_target="tpu_custom_call", output_to_operand_aliasing={{}: (2, {})} | custom-call | flops 40000000000 | bytes 2359296 | tf_op jit(solution)/shard_map/stage3/pallas_call | solution.py:192
  206.1 3.6 %copy-done = f32[1536,1536]{1,0:T(8,128)} copy-done((f32[1536,1536]{1,0:T(8,128)}, f32[1536,1536]{1,0:T(8,128)S(1)}, u32[]{:S(2)}) %copy-start) | copy-done | bytes 9437208
  209.6 3.7 %copy-done.1 = f32[1536,1536]{1,0:T(8,128)S(1)} copy-done((f32[1536,1536]{1,0:T(8,128)S(1)}, f32[1536,1536]{1,0:T(8,128)}, u32[]{:S(2)}) %copy-start.1) | copy-done | bytes 9437208
  213.3 3.9 %copy-done.2 = f32[1536,1664]{1,0:T(8,128)S(1)} copy-done((f32[1536,1664]{1,0:T(8,128)S(1)}, f32[1536,1664]{1,0:T(8,128)}, u32[]{:S(2)}) %copy-start.2) | copy-done | bytes 10223640
  218.2 0.7 collective-permute-start.8
  218.9 0.8 collective-permute-start.9
  219.8 0.8 collective-permute-start.10
  221.0 1.3 slice-done.1
  222.6 3.9 %gains.1 = f32[48,1536]{1,0:T(8,128)} custom-call(f32[48,1536]{1,0:T(8,128)S(1)} %bitcast.26, f32[1536,1536]{1,0:T(8,128)S(1)} %bitcast.22), custom_call_target="tpu_custom_call" | custom-call | flops 1000000000 | bytes 9437184 | tf_op jit(solution)/shard_map/gains/pallas_call | solution.py:179
  227.2 1.3 collective-permute-start.12
  228.5 24.4 %collective-permute-done.12.refs_0_ = f32[1,1536]{1,0:T(1,128)S(1)} collective-permute-done((f32[1,1536]{1,0:T(1,128)S(1)}, f32[1,1536]{1,0:T(1,128)S(1)}, u32[]{:S(2)}, u32[]{:S(2)}) %collective-permute-start.12) | collective-permute-done | bytes 6176 | tf_op jit(solution)/shard_map/ppermute | solution.py:307
  252.9 2.0 turn6.1.refs_1_
  255.0 1.3 collective-permute-start.13
  256.3 0.8 collective-permute-done.13.refs_0_
  (48 shorter events, 4.5 us)
Async XLA Ops:
  7.2 202.5 %all-gather.2.cloned.1.call-start = ((), (), s32[]{:S(2)}) async-start(), calls=%async_computation | async-start | bytes 10543104 | tf_op jit(solution)/shard_map/all_gather | solution.py:292
  7.2 5.4 %collective-permute-start = (bf16[48,1536]{1,0:T(8,128)(2,1)}, bf16[48,1536]{1,0:T(8,128)(2,1)S(1)}, u32[]{:S(2)}, u32[]{:S(2)}) collective-permute-start(bf16[48,1536]{1,0:T(8,128)(2,1)} %bitcast.27), channel_id=1, source_target_pairs={{0,4},{1,5},{2,6},{3,7},{4,0},{5,1},{6,2},{7,3},{8,12},{9,13},{10,... | collective-permute-start | bytes 442376 | tf_op jit(solution)/shard_map/ppermute | solution.py:271
  13.5 10.1 %collective-permute-start.1 = (bf16[96,1536]{1,0:T(8,128)(2,1)S(1)}, bf16[96,1536]{1,0:T(8,128)(2,1)S(1)}, u32[]{:S(2)}, u32[]{:S(2)}) collective-permute-start(bf16[96,1536]{1,0:T(8,128)(2,1)S(1)} %pad_maximum_fusion), channel_id=1, source_target_pairs={{1,0},{2,1},{3,2},{0,3},{5,4},{6,5},{7,6},{4,7},{9,8},{10,9},{11,1... | collective-permute-start | bytes 884744 | tf_op jit(solution)/shard_map/ppermute | solution.py:275
  18.9 8.5 %collective-permute-start.2 = (bf16[96,1536]{1,0:T(8,128)(2,1)S(1)}, bf16[96,1536]{1,0:T(8,128)(2,1)S(1)}, u32[]{:S(2)}, u32[]{:S(2)}) collective-permute-start(bf16[96,1536]{1,0:T(8,128)(2,1)S(1)} %pad_maximum_fusion), channel_id=1, source_target_pairs={{2,0},{3,1},{0,2},{1,3},{6,4},{7,5},{4,6},{5,7},{10,8},{11,9},{8,1... | collective-permute-start | bytes 884744 | tf_op jit(solution)/shard_map/ppermute | solution.py:275
  19.2 16.4 %collective-permute-start.3 = (bf16[96,1536]{1,0:T(8,128)(2,1)S(1)}, bf16[96,1536]{1,0:T(8,128)(2,1)S(1)}, u32[]{:S(2)}, u32[]{:S(2)}) collective-permute-start(bf16[96,1536]{1,0:T(8,128)(2,1)S(1)} %pad_maximum_fusion), channel_id=1, source_target_pairs={{3,0},{0,1},{1,2},{2,3},{7,4},{4,5},{5,6},{6,7},{11,8},{8,9},{9,10... | collective-permute-start | bytes 884744 | tf_op jit(solution)/shard_map/ppermute | solution.py:275
  36.3 42.8 %collective-permute-start.4 = (bf16[384,1536]{1,0:T(8,128)(2,1)S(1)}, bf16[384,1536]{1,0:T(8,128)(2,1)S(1)}, u32[]{:S(2)}, u32[]{:S(2)}) collective-permute-start(bf16[384,1536]{1,0:T(8,128)(2,1)S(1)} %constant_dynamic-update-slice_fusion.block_ref), channel_id=1, source_target_pairs={{0,28},{1,29},{2,30},{3,31},{4,8},{5,9},{6,10},{7,11},{8,4},{9,5},... | collective-permute-start | bytes 3538952 | tf_op jit(solution)/shard_map/ppermute | solution.py:271
  79.1 40.3 %collective-permute-start.5 = (bf16[384,1536]{1,0:T(8,128)(2,1)S(1)}, bf16[384,1536]{1,0:T(8,128)(2,1)S(1)}, u32[]{:S(2)}, u32[]{:S(2)}) collective-permute-start(bf16[384,1536]{1,0:T(8,128)(2,1)S(1)} %collective-permute-done.4.block_ref), channel_id=1, source_target_pairs={{0,4},{1,5},{2,6},{3,7},{4,0},{5,1},{6,2},{7,3},{8,12},{9,13},{10,... | collective-permute-start | bytes 3538952 | tf_op jit(solution)/shard_map/ppermute | solution.py:271
  119.4 52.1 %collective-permute-start.6 = (bf16[384,1536]{1,0:T(8,128)(2,1)S(1)}, bf16[384,1536]{1,0:T(8,128)(2,1)S(1)}, u32[]{:S(2)}, u32[]{:S(2)}) collective-permute-start(bf16[384,1536]{1,0:T(8,128)(2,1)S(1)} %collective-permute-done.5.block_ref), channel_id=1, source_target_pairs={{0,28},{1,29},{2,30},{3,31},{4,8},{5,9},{6,10},{7,11},{8,4},{9,5},... | collective-permute-start | bytes 3538952 | tf_op jit(solution)/shard_map/ppermute | solution.py:271
  206.0 3.6 %copy-start = (f32[1536,1536]{1,0:T(8,128)}, f32[1536,1536]{1,0:T(8,128)S(1)}, u32[]{:S(2)}) copy-start(f32[1536,1536]{1,0:T(8,128)S(1)} %stage3.1.refs_0_.refs_4_.w_ref) | copy-start | bytes 28311556
  209.6 3.7 %copy-start.1 = (f32[1536,1536]{1,0:T(8,128)S(1)}, f32[1536,1536]{1,0:T(8,128)}, u32[]{:S(2)}) copy-start(f32[1536,1536]{1,0:T(8,128)} %copy-done) | copy-start | bytes 28311556
  213.3 3.9 %copy-start.2 = (f32[1536,1664]{1,0:T(8,128)S(1)}, f32[1536,1664]{1,0:T(8,128)}, u32[]{:S(2)}) copy-start(f32[1536,1664]{1,0:T(8,128)} %all-gather.2.cloned.1.call-done.refs_1_.refs_5_) | copy-start | bytes 30670852
  217.5 0.7 collective-permute-start.7
  218.2 0.7 collective-permute-start.8
  218.8 2.2 slice-start
  218.9 3.5 %slice-start.1 = ((s8[9437184]{0:T(1024)(128)(4,1)}), s8[4194304]{0:T(1024)(128)(4,1)S(1)}, s32[]{:S(2)}) async-start(s8[9437184]{0:T(1024)(128)(4,1)} %bitcast.21), calls=%async_computation.2 | async-start | bytes 8388608
  218.9 3.6 %slice-start.2 = ((s8[9437184]{0:T(1024)(128)(4,1)}), s8[1048576]{0:T(1024)(128)(4,1)S(1)}, s32[]{:S(2)}) async-start(s8[9437184]{0:T(1024)(128)(4,1)} %bitcast.21), calls=%async_computation.3 | async-start | bytes 2097152
  218.9 3.7 %copy-start.3 = (f32[1,48,1536]{2,1,0:T(8,128)S(1)}, f32[1,48,1536]{2,1,0:T(8,128)}, u32[]{:S(2)}) copy-start(f32[1,48,1536]{2,1,0:T(8,128)} %param.6) | copy-start | bytes 884740
  218.9 0.8 collective-permute-start.9
  219.7 6.7 %slice-start.3 = ((s8[10223616]{0:T(1024)(128)(4,1)}), s8[4194304]{0:T(1024)(128)(4,1)S(1)}, s32[]{:S(2)}) async-start(s8[10223616]{0:T(1024)(128)(4,1)} %bitcast.23), calls=%async_computation.4 | async-start | bytes 8388608
  219.7 6.7 %slice-start.4 = ((s8[10223616]{0:T(1024)(128)(4,1)}), s8[4194304]{0:T(1024)(128)(4,1)S(1)}, s32[]{:S(2)}) async-start(s8[10223616]{0:T(1024)(128)(4,1)} %bitcast.23), calls=%async_computation.5 | async-start | bytes 8388608
  219.8 6.7 %slice-start.5 = ((s8[10223616]{0:T(1024)(128)(4,1)}), s8[1835008]{0:T(1024)(128)(4,1)S(1)}, s32[]{:S(2)}) async-start(s8[10223616]{0:T(1024)(128)(4,1)} %bitcast.23), calls=%async_computation.6 | async-start | bytes 3670016
  219.8 6.7 %collective-permute-start.10 = (f32[1,1536]{1,0:T(1,128)S(1)}, f32[1,1536]{1,0:T(1,128)S(1)}, u32[]{:S(2)}, u32[]{:S(2)}) collective-permute-start(f32[1,1536]{1,0:T(1,128)S(1)} %turn3.1.refs_1_), channel_id=1, source_target_pairs={{128,96},{129,97},{130,98},{131,99},{132,100},{133,101},{134,102},... | collective-permute-start | bytes 18440 | tf_op jit(solution)/shard_map/ppermute | solution.py:307
  226.5 0.7 collective-permute-start.11
  227.2 25.7 %collective-permute-start.12 = (f32[1,1536]{1,0:T(1,128)S(1)}, f32[1,1536]{1,0:T(1,128)S(1)}, u32[]{:S(2)}, u32[]{:S(2)}) collective-permute-start(f32[1,1536]{1,0:T(1,128)S(1)} %turn5.1.refs_1_), channel_id=1, source_target_pairs={{64,32},{65,33},{66,34},{67,35},{68,36},{69,37},{70,38},{71,39},{7... | collective-permute-start | bytes 18440 | tf_op jit(solution)/shard_map/ppermute | solution.py:307
  255.0 2.1 collective-permute-start.13
Sparse Core Ops, SparseCore 0:
  35.8 142.0 all-gather.1
where the time goes:
time: 265 us; the launch traced here: 264 us
  Pallas kernels  118 us (45%)
  waiting for transfers between devices  93.8 us (35%)
  starting transfers between devices  19.3 us (7%)
  local copies, waits for them, and re-layouts  15.2 us (6%)
  between operations  14.6 us (6%)
  other arithmetic  3.34 us (1%)
    pallas_call x4, Pallas kernels, sweep_stage(): pl.pallas_call(functools.partial(stage_kernel, stage), name='stage' + str...  112 us
    ppermute x4, waiting for transfers between devices, swap(): return lax.ppermute(x, 'row', pairs)  52.9 us
    ppermute x7, waiting for transfers between devices, per_device(): late = lax.ppermute(state, 'tm', [(steps - n, steps - n - 1)])  25.2 us
    ppermute x3, waiting for transfers between devices, along_y(): lax.ppermute(x, 'row', [(z * Y + (y + d) % Y, z * Y + y) for z in range(Z...  15.7 us
    unnamed x24, local copies, waits for them, and re-layouts  14.2 us
    ppermute x4, starting transfers between devices, swap(): return lax.ppermute(x, 'row', pairs)  8.43 us
    ppermute x7, starting transfers between devices, per_device(): late = lax.ppermute(state, 'tm', [(steps - n, steps - n - 1)])  6.15 us
  transfers between devices with their start and end apart: 15, of which 9 were waited for; matrix products, arithmetic and copies ran while one was open for 1% of the time, Pallas kernels for 44%

commit v1 on v0

--- a/solution.py
+++ b/solution.py
@@ -96,17 +96,10 @@
     lax.fori_loop(0, B // H, step, 0)
 
 
-def stage_kernel(stage, ids, block_ref, *refs):
-    if stage:
-        _, *refs = refs
-    w_ref, p_ref, t3_ref, d_ref, m_ref, r_ref = refs
+def stage_kernel(stage, ids, *refs):
+    before_ref, w_ref, p_ref, t3_ref, d_ref, m_ref, r_ref = refs[Y:]
     here = pl.multiple_of(ids[stage] * B, B)
-    for n in range(2):
-        for d in range(Y):
-            y = lax.rem(ids[6] + d, Y)
-            to = pl.multiple_of(lax.rem(ids[4 + n], 2) * PIECE + y * MINE, 16)
-            at = (2 * d + n) * MINE
-            p_ref[pl.ds(to, MINE), :] = block_ref[at : at + MINE, :]
+    place(ids, refs[:Y], p_ref)
     rows = pl.ds(here, B)
     w_ref[rows, :] = p_ref[...].astype(f32)
     if stage:
@@ -131,8 +124,11 @@
             return lax.fori_loop(0, N // TILE, tile, 0)
 
         lax.fori_loop(0, stage, earlier, 0)
-    d_ref[...] = w_ref[rows, pl.ds(here, B)]
-    block_sweep(d_ref, m_ref, r_ref)
+    if stage:
+        d_ref[...] = w_ref[rows, pl.ds(here, B)]
+        block_sweep(d_ref, m_ref, r_ref)
+    else:
+        d_ref[...] = before_ref[...]
     minus = d_ref[...]
     left = wide(minus)
 
@@ -187,13 +183,39 @@
     )(cross, minus_inverse)
 
 
-def sweep_stage(stage, ids, block, w):
-    args = [ids, block] + ([w] if stage else [])
+def place(ids, refs, to_ref):
+    for d, ref in enumerate(refs):
+        for n in range(2):
+            y = lax.rem(ids[6] + d, Y)
+            to = pl.multiple_of(lax.rem(ids[4 + n], 2) * PIECE + y * MINE, 16)
+            to_ref[pl.ds(to, MINE), :] = ref[n * MINE : (n + 1) * MINE, :].astype(to_ref.dtype)
+
+
+def own_block_kernel(ids, *refs):
+    d_ref, m_ref, r_ref = refs[Y:]
+    place(ids, refs[:Y], d_ref)
+    block_sweep(d_ref, m_ref, r_ref)
+
+
+def own_block(ids, pieces):
+    return pl.pallas_call(
+        own_block_kernel,
+        name="own_block",
+        out_shape=jax.ShapeDtypeStruct((B, B), f32),
+        in_specs=[SMEM_WHOLE] + [VMEM_WHOLE] * Y,
+        out_specs=VMEM_WHOLE,
+        scratch_shapes=[pltpu.VMEM((H, H), f32), pltpu.VMEM((B, H), f32)],
+        compiler_params=pltpu.CompilerParams(vmem_limit_bytes=8 << 20),
+        cost_estimate=pl.CostEstimate(flops=20_000_000_000, bytes_accessed=2 * B * B, transcendentals=0),
+    )(ids, *pieces)
+
+
+def sweep_stage(stage, ids, pieces, before):
     return pl.pallas_call(
         functools.partial(stage_kernel, stage),
         name="stage" + str(stage),
         out_shape=jax.ShapeDtypeStruct((N, N), f32),
-        in_specs=[SMEM_WHOLE] + [VMEM_WHOLE] * (len(args) - 1),
+        in_specs=[SMEM_WHOLE] + [VMEM_WHOLE] * (Y + 1),
         out_specs=VMEM_WHOLE,
         scratch_shapes=[
             pltpu.VMEM((B, N), bf16),
@@ -202,10 +224,10 @@
             pltpu.VMEM((H, H), f32),
             pltpu.VMEM((B, H), f32),
         ],
-        input_output_aliases={2: 0} if stage else {},
+        input_output_aliases={Y + 1: 0} if stage else {},
         compiler_params=pltpu.CompilerParams(vmem_limit_bytes=STAGE_VMEM),
         cost_estimate=pl.CostEstimate(flops=40_000_000_000, bytes_accessed=4 * B * N, transcendentals=0),
-    )(*args)
+    )(ids, *pieces, before)
 
 
 STAGE_VMEM = 24 << 20
@@ -285,22 +307,28 @@
     mine = (steps - 1 - lax.axis_index("tm")).astype(jnp.int32)[None]
     pred_cov, first, mine = lax.optimization_barrier((pred_cov, first, mine))
 
-    pair = jnp.concatenate([pred_cov[0], swap(pred_cov[0], True)], axis=0)
-    pairs = [pair] + [along_y(pair, d) for d in range(1, Y)]
-    own = jnp.concatenate(pairs, axis=0)
-    packed, own = lax.optimization_barrier((packed, own))
+    def along_all_y(x):
+        return [x] + [along_y(x, d) for d in range(1, Y)]
+
+    def strips(x):
+        return jnp.concatenate([x, swap(x, True)], axis=0)
+
+    diagonal = lax.dynamic_slice(pred_cov[0], (jnp.uint32(0), (z // 2 * B).astype(jnp.uint32)), (MINE, B))
+    diagonal, rest = lax.optimization_barrier((strips(diagonal), pred_cov[0]))
+    diagonal = along_all_y(diagonal)
+    strip0, packed = lax.optimization_barrier((strips(rest), packed))
     packed = lax.all_gather(packed, "row", axis=0, tiled=True)
-    block1 = swap(own, False)
-    block2 = swap(block1, True)
-    block3 = swap(block2, False)
+    strip1 = swap(strip0, False)
+    strip2 = swap(strip1, True)
+    strip3 = swap(strip2, False)
     e = 1 - 2 * (z % 2)
     at = lambda k: (z + e * k + Z) % Z
     order = [at(0) // 2, at(-1) // 2, at(2) // 2, at(-3) // 2]
     ids = lambda m, n: jnp.stack(order + [at(m), at(n), y, y]).astype(jnp.int32)
-    w = sweep_stage(0, ids(0, 1), own, None)
-    w = sweep_stage(1, ids(-1, -2), block1, w)
-    w = sweep_stage(2, ids(2, 3), block2, w)
-    w = sweep_stage(3, ids(-3, -4), block3, w)
+    w = sweep_stage(0, ids(0, 1), along_all_y(strip0), own_block(ids(0, 1), diagonal))
+    w = sweep_stage(1, ids(-1, -2), along_all_y(strip1), w)
+    w = sweep_stage(2, ids(2, 3), along_all_y(strip2), w)
+    w = sweep_stage(3, ids(-3, -4), along_all_y(strip3), w)
 
     state, base, mean = turn(0, mine, w, packed)
     for n in range(1, steps):

time: 265 us -> 235 us (0.89)
  the two profiles are of different devices: /device:TPU:1 before, /device:TPU:16 now
where the time goes in v1:
time: 235 us; the launch traced here: 230 us
  Pallas kernels  119 us (51%)
  starting transfers between devices  49.2 us (21%)
  waiting for transfers between devices  29.3 us (12%)
  local copies, waits for them, and re-layouts  15.1 us (6%)
  between operations  14.6 us (6%)
  other arithmetic  3.35 us (1%)
    pallas_call x4, Pallas kernels, sweep_stage(): pl.pallas_call(functools.partial(stage_kernel, stage), name='stage' + str...  93.4 us
    ppermute x15, starting transfers between devices, along_y(): lax.ppermute(x, 'row', [(z * Y + (y + d) % Y, z * Y + y) for z in range(Z...  31.2 us
    ppermute x7, waiting for transfers between devices, per_device(): late = lax.ppermute(state, 'tm', [(steps - n, steps - n - 1)])  22.1 us
    pallas_call x1, Pallas kernels, own_block(): pl.pallas_call(own_block_kernel, name='own_block', out_shape=jax.ShapeDty...  19 us
    unnamed x20, local copies, waits for them, and re-layouts  13.2 us
    ppermute x5, starting transfers between devices, swap(): return lax.ppermute(x, 'row', pairs)  12.5 us
    ppermute x5, waiting for transfers between devices, swap(): return lax.ppermute(x, 'row', pairs)  7.18 us
    ppermute x7, starting transfers between devices, per_device(): late = lax.ppermute(state, 'tm', [(steps - n, steps - n - 1)])  5.52 us
  transfers between devices with their start and end apart: 28, of which 4 were waited for; matrix products, arithmetic and copies ran while one was open for 1% of the time, Pallas kernels for 50%

profile of v1, /device:TPU:16, one launch (start us, length us, event | category | flops | bytes accessed | tf_op | source)
XLA Modules:
  0.0 230.2 jit_solution(13397689093325567105)
XLA Ops:
  7.3 0.9 dynamic-slice_bitcast_fusion
  8.1 2.0 collective-permute-start
  10.9 1.3 collective-permute-done
  12.2 2.0 collective-permute-start.1
  14.2 1.7 select_maximum_fusion
  15.9 1.7 collective-permute-done.1
  17.6 0.9 pad_maximum_fusion.refs_0_
  19.1 2.9 %collective-permute-start.18 = (bf16[96,384]{1,0:T(8,128)(2,1)S(1)}, bf16[96,384]{1,0:T(8,128)(2,1)S(1)}, u32[]{:S(2)}, u32[]{:S(2)}) collective-permute-start(bf16[96,384]{1,0:T(8,128)(2,1)S(1)} %pad_maximum_fusion.1.refs_0_), channel_id=1, source_target_pairs={{2,0},{3,1},{0,2},{1,3},{6,4},{7,5},{4,6},{5,7},{10,8},{11,9},{8,1... | collective-permute-start | bytes 221192 | tf_op jit(solution)/shard_map/ppermute | solution.py:297
  22.0 1.4 collective-permute-start.19
  24.4 1.8 collective-permute-start.15
  26.6 6.0 %collective-permute-start.2 = (bf16[96,1536]{1,0:T(8,128)(2,1)S(1)}, bf16[96,1536]{1,0:T(8,128)(2,1)S(1)}, u32[]{:S(2)}, u32[]{:S(2)}) collective-permute-start(bf16[96,1536]{1,0:T(8,128)(2,1)S(1)} %pad_maximum_fusion.refs_0_), channel_id=1, source_target_pairs={{0,28},{1,29},{2,30},{3,31},{4,8},{5,9},{6,10},{7,11},{8,4},{9,5},... | collective-permute-start | bytes 884744 | tf_op jit(solution)/shard_map/ppermute | solution.py:293
  32.6 19.0 %own_block.1.refs_4_ = f32[384,384]{1,0:T(8,128)S(1)} custom-call(s32[8]{0:T(128)S(1)} %stack.103.ids, bf16[96,384]{1,0:T(8,128)(2,1)S(1)} %pad_maximum_fusion.1.refs_0_, bf16[96,384]{1,0:T(8,128)(2,1)S(1)} %collective-permute-done.17.refs_1_, bf16[96,384]{1,0:T(8,128)(2,1)S(1)} %collective-permute-done.18.refs_2_, ...), custom_call_target="tpu_custom_call" | custom-call | flops 20000000000 | bytes 294912 | tf_op jit(solution)/shard_map/own_block/pallas_call | solution.py:201
  51.6 1.6 collective-permute-start.11
  53.1 2.9 %collective-permute-start.12 = (bf16[96,1536]{1,0:T(8,128)(2,1)S(1)}, bf16[96,1536]{1,0:T(8,128)(2,1)S(1)}, u32[]{:S(2)}, u32[]{:S(2)}) collective-permute-start(bf16[96,1536]{1,0:T(8,128)(2,1)S(1)} %collective-permute-done.2.refs_0_), channel_id=1, source_target_pairs={{2,0},{3,1},{0,2},{1,3},{6,4},{7,5},{4,6},{5,7},{10,8},{11,9},{8,1... | collective-permute-start | bytes 884744 | tf_op jit(solution)/shard_map/ppermute | solution.py:297
  56.9 3.0 %stage0.1.refs_4_ = f32[1536,1536]{1,0:T(8,128)S(1)} custom-call(s32[8]{0:T(128)S(1)} %stack.103.ids, bf16[96,1536]{1,0:T(8,128)(2,1)S(1)} %pad_maximum_fusion.refs_0_, bf16[96,1536]{1,0:T(8,128)(2,1)S(1)} %collective-permute-done.14.refs_1_, bf16[96,1536]{1,0:T(8,128)(2,1)S(1)} %collective-permute-done.15.refs_2_, ...), custom_call_target="tpu_custom_call" | custom-call | flops 40000000000 | bytes 2359296 | tf_op jit(solution)/shard_map/stage0/pallas_call | solution.py:214
  60.0 4.2 %collective-permute-done.3.refs_0_ = bf16[96,1536]{1,0:T(8,128)(2,1)S(1)} collective-permute-done((bf16[96,1536]{1,0:T(8,128)(2,1)S(1)}, bf16[96,1536]{1,0:T(8,128)(2,1)S(1)}, u32[]{:S(2)}, u32[]{:S(2)}) %collective-permute-start.3) | collective-permute-done | bytes 294944 | tf_op jit(solution)/shard_map/ppermute | solution.py:293
  64.2 1.8 collective-permute-start.10
  66.2 2.9 %collective-permute-start.9 = (bf16[96,1536]{1,0:T(8,128)(2,1)S(1)}, bf16[96,1536]{1,0:T(8,128)(2,1)S(1)}, u32[]{:S(2)}, u32[]{:S(2)}) collective-permute-start(bf16[96,1536]{1,0:T(8,128)(2,1)S(1)} %collective-permute-done.3.refs_0_), channel_id=1, source_target_pairs={{2,0},{3,1},{0,2},{1,3},{6,4},{7,5},{4,6},{5,7},{10,8},{11,9},{8,1... | collective-permute-start | bytes 884744 | tf_op jit(solution)/shard_map/ppermute | solution.py:297
  69.1 2.1 collective-permute-start.4
  71.2 25.8 %stage1.1.refs_4_ = f32[1536,1536]{1,0:T(8,128)S(1)} custom-call(s32[8]{0:T(128)S(1)} %stack.100.ids, bf16[96,1536]{1,0:T(8,128)(2,1)S(1)} %collective-permute-done.2.refs_0_, bf16[96,1536]{1,0:T(8,128)(2,1)S(1)} %collective-permute-done.11.refs_1_, bf16[96,1536]{1,0:T(8,128)(2,1)S(1)} %collective-permute-done.12.refs_2_, ...), custom_call_target="tpu_custom_call", output_to_operand_aliasing={{}: (5, {})} | custom-call | flops 40000000000 | bytes 2359296 | tf_op jit(solution)/shard_map/stage1/pallas_call | solution.py:214
  97.4 11.3 %collective-permute-start.6 = (bf16[96,1536]{1,0:T(8,128)(2,1)S(1)}, bf16[96,1536]{1,0:T(8,128)(2,1)S(1)}, u32[]{:S(2)}, u32[]{:S(2)}) collective-permute-start(bf16[96,1536]{1,0:T(8,128)(2,1)S(1)} %collective-permute-done.4.refs_0_), channel_id=1, source_target_pairs={{2,0},{3,1},{0,2},{1,3},{6,4},{7,5},{4,6},{5,7},{10,8},{11,9},{8,1... | collective-permute-start | bytes 884744 | tf_op jit(solution)/shard_map/ppermute | solution.py:297
  108.6 2.0 collective-permute-start.7
  110.6 30.0 %stage2.1.refs_4_ = f32[1536,1536]{1,0:T(8,128)S(1)} custom-call(s32[8]{0:T(128)S(1)} %stack.97.ids, bf16[96,1536]{1,0:T(8,128)(2,1)S(1)} %collective-permute-done.3.refs_0_, bf16[96,1536]{1,0:T(8,128)(2,1)S(1)} %collective-permute-done.8.refs_1_, bf16[96,1536]{1,0:T(8,128)(2,1)S(1)} %collective-permute-done.9.refs_2_, ...), custom_call_target="tpu_custom_call", output_to_operand_aliasing={{}: (5, {})} | custom-call | flops 40000000000 | bytes 2359296 | tf_op jit(solution)/shard_map/stage2/pallas_call | solution.py:214
  140.7 34.5 %stage3.1.refs_0_.refs_4_.w_ref = f32[1536,1536]{1,0:T(8,128)S(1)} custom-call(s32[8]{0:T(128)S(1)} %stack.45.ids, bf16[96,1536]{1,0:T(8,128)(2,1)S(1)} %collective-permute-done.4.refs_0_, bf16[96,1536]{1,0:T(8,128)(2,1)S(1)} %collective-permute-done.5.refs_1_, bf16[96,1536]{1,0:T(8,128)(2,1)S(1)} %collective-permute-done.6.refs_2_, ...), custom_call_target="tpu_custom_call", output_to_operand_aliasing={{}: (5, {})} | custom-call | flops 40000000000 | bytes 2359296 | tf_op jit(solution)/shard_map/stage3/pallas_call | solution.py:214
  175.3 3.6 %copy-done = f32[1536,1536]{1,0:T(8,128)} copy-done((f32[1536,1536]{1,0:T(8,128)}, f32[1536,1536]{1,0:T(8,128)S(1)}, u32[]{:S(2)}) %copy-start) | copy-done | bytes 9437208
  178.8 3.7 %copy-done.1 = f32[1536,1536]{1,0:T(8,128)S(1)} copy-done((f32[1536,1536]{1,0:T(8,128)S(1)}, f32[1536,1536]{1,0:T(8,128)}, u32[]{:S(2)}) %copy-start.1) | copy-done | bytes 9437208
  182.5 3.9 %copy-done.2 = f32[1536,1664]{1,0:T(8,128)S(1)} copy-done((f32[1536,1664]{1,0:T(8,128)S(1)}, f32[1536,1664]{1,0:T(8,128)}, u32[]{:S(2)}) %copy-start.2) | copy-done | bytes 10223640
  190.2 1.3 slice-done.1
  191.8 3.9 %gains.1 = f32[48,1536]{1,0:T(8,128)} custom-call(f32[48,1536]{1,0:T(8,128)S(1)} %bitcast.27, f32[1536,1536]{1,0:T(8,128)S(1)} %bitcast.23), custom_call_target="tpu_custom_call" | custom-call | flops 1000000000 | bytes 9437184 | tf_op jit(solution)/shard_map/gains/pallas_call | solution.py:175
  197.1 1.3 collective-permute-start.26
  198.4 22.1 %collective-permute-done.26.refs_0_ = f32[1,1536]{1,0:T(1,128)S(1)} collective-permute-done((f32[1,1536]{1,0:T(1,128)S(1)}, f32[1,1536]{1,0:T(1,128)S(1)}, u32[]{:S(2)}, u32[]{:S(2)}) %collective-permute-start.26) | collective-permute-done | bytes 6176 | tf_op jit(solution)/shard_map/ppermute | solution.py:335
  220.5 2.0 turn7.1
  (72 shorter events, 10.2 us)
Async XLA Ops:
  7.2 171.7 %all-gather.2.cloned.1.call-start = ((), (), s32[]{:S(2)}) async-start(), calls=%async_computation | async-start | bytes 10543104 | tf_op jit(solution)/shard_map/all_gather | solution.py:320
  8.1 4.0 %collective-permute-start = (bf16[48,384]{1,0:T(8,128)(2,1)S(1)}, bf16[48,384]{1,0:T(8,128)(2,1)S(1)}, u32[]{:S(2)}, u32[]{:S(2)}) collective-permute-start(bf16[48,384]{1,0:T(8,128)(2,1)S(1)} %dynamic-slice_bitcast_fusion), channel_id=1, source_target_pairs={{0,4},{1,5},{2,6},{3,7},{4,0},{5,1},{6,2},{7,3},{8,12},{9,13},{10,... | collective-permute-start | bytes 110600 | tf_op jit(solution)/shard_map/ppermute | solution.py:293
  12.2 5.4 %collective-permute-start.1 = (bf16[48,1536]{1,0:T(8,128)(2,1)}, bf16[48,1536]{1,0:T(8,128)(2,1)S(1)}, u32[]{:S(2)}, u32[]{:S(2)}) collective-permute-start(bf16[48,1536]{1,0:T(8,128)(2,1)} %bitcast.29), channel_id=1, source_target_pairs={{0,4},{1,5},{2,6},{3,7},{4,0},{5,1},{6,2},{7,3},{8,12},{9,13},{10,... | collective-permute-start | bytes 442376 | tf_op jit(solution)/shard_map/ppermute | solution.py:293
  18.6 7.7 %collective-permute-start.17 = (bf16[96,384]{1,0:T(8,128)(2,1)S(1)}, bf16[96,384]{1,0:T(8,128)(2,1)S(1)}, u32[]{:S(2)}, u32[]{:S(2)}) collective-permute-start(bf16[96,384]{1,0:T(8,128)(2,1)S(1)} %pad_maximum_fusion.1.refs_0_), channel_id=1, source_target_pairs={{1,0},{2,1},{3,2},{0,3},{5,4},{6,5},{7,6},{4,7},{9,8},{10,9},{11,1... | collective-permute-start | bytes 221192 | tf_op jit(solution)/shard_map/ppermute | solution.py:297
  19.1 7.5 %collective-permute-start.18 = (bf16[96,384]{1,0:T(8,128)(2,1)S(1)}, bf16[96,384]{1,0:T(8,128)(2,1)S(1)}, u32[]{:S(2)}, u32[]{:S(2)}) collective-permute-start(bf16[96,384]{1,0:T(8,128)(2,1)S(1)} %pad_maximum_fusion.1.refs_0_), channel_id=1, source_target_pairs={{2,0},{3,1},{0,2},{1,3},{6,4},{7,5},{4,6},{5,7},{10,8},{11,9},{8,1... | collective-permute-start | bytes 221192 | tf_op jit(solution)/shard_map/ppermute | solution.py:297
  22.0 10.6 %collective-permute-start.19 = (bf16[96,384]{1,0:T(8,128)(2,1)S(1)}, bf16[96,384]{1,0:T(8,128)(2,1)S(1)}, u32[]{:S(2)}, u32[]{:S(2)}) collective-permute-start(bf16[96,384]{1,0:T(8,128)(2,1)S(1)} %pad_maximum_fusion.1.refs_0_), channel_id=1, source_target_pairs={{3,0},{0,1},{1,2},{2,3},{7,4},{4,5},{5,6},{6,7},{11,8},{8,9},{9,10... | collective-permute-start | bytes 221192 | tf_op jit(solution)/shard_map/ppermute | solution.py:297
  23.7 32.4 %collective-permute-start.14 = (bf16[96,1536]{1,0:T(8,128)(2,1)S(1)}, bf16[96,1536]{1,0:T(8,128)(2,1)S(1)}, u32[]{:S(2)}, u32[]{:S(2)}) collective-permute-start(bf16[96,1536]{1,0:T(8,128)(2,1)S(1)} %pad_maximum_fusion.refs_0_), channel_id=1, source_target_pairs={{1,0},{2,1},{3,2},{0,3},{5,4},{6,5},{7,6},{4,7},{9,8},{10,9},{11,1... | collective-permute-start | bytes 884744 | tf_op jit(solution)/shard_map/ppermute | solution.py:297
  24.4 32.1 %collective-permute-start.15 = (bf16[96,1536]{1,0:T(8,128)(2,1)S(1)}, bf16[96,1536]{1,0:T(8,128)(2,1)S(1)}, u32[]{:S(2)}, u32[]{:S(2)}) collective-permute-start(bf16[96,1536]{1,0:T(8,128)(2,1)S(1)} %pad_maximum_fusion.refs_0_), channel_id=1, source_target_pairs={{2,0},{3,1},{0,2},{1,3},{6,4},{7,5},{4,6},{5,7},{10,8},{11,9},{8,1... | collective-permute-start | bytes 884744 | tf_op jit(solution)/shard_map/ppermute | solution.py:297
  26.2 30.7 %collective-permute-start.16 = (bf16[96,1536]{1,0:T(8,128)(2,1)S(1)}, bf16[96,1536]{1,0:T(8,128)(2,1)S(1)}, u32[]{:S(2)}, u32[]{:S(2)}) collective-permute-start(bf16[96,1536]{1,0:T(8,128)(2,1)S(1)} %pad_maximum_fusion.refs_0_), channel_id=1, source_target_pairs={{3,0},{0,1},{1,2},{2,3},{7,4},{4,5},{5,6},{6,7},{11,8},{8,9},{9,10... | collective-permute-start | bytes 884744 | tf_op jit(solution)/shard_map/ppermute | solution.py:297
  26.6 24.9 %collective-permute-start.2 = (bf16[96,1536]{1,0:T(8,128)(2,1)S(1)}, bf16[96,1536]{1,0:T(8,128)(2,1)S(1)}, u32[]{:S(2)}, u32[]{:S(2)}) collective-permute-start(bf16[96,1536]{1,0:T(8,128)(2,1)S(1)} %pad_maximum_fusion.refs_0_), channel_id=1, source_target_pairs={{0,28},{1,29},{2,30},{3,31},{4,8},{5,9},{6,10},{7,11},{8,4},{9,5},... | collective-permute-start | bytes 884744 | tf_op jit(solution)/shard_map/ppermute | solution.py:293
  51.6 14.6 %collective-permute-start.11 = (bf16[96,1536]{1,0:T(8,128)(2,1)S(1)}, bf16[96,1536]{1,0:T(8,128)(2,1)S(1)}, u32[]{:S(2)}, u32[]{:S(2)}) collective-permute-start(bf16[96,1536]{1,0:T(8,128)(2,1)S(1)} %collective-permute-done.2.refs_0_), channel_id=1, source_target_pairs={{1,0},{2,1},{3,2},{0,3},{5,4},{6,5},{7,6},{4,7},{9,8},{10,9},{11,1... | collective-permute-start | bytes 884744 | tf_op jit(solution)/shard_map/ppermute | solution.py:297
  53.1 16.0 %collective-permute-start.12 = (bf16[96,1536]{1,0:T(8,128)(2,1)S(1)}, bf16[96,1536]{1,0:T(8,128)(2,1)S(1)}, u32[]{:S(2)}, u32[]{:S(2)}) collective-permute-start(bf16[96,1536]{1,0:T(8,128)(2,1)S(1)} %collective-permute-done.2.refs_0_), channel_id=1, source_target_pairs={{2,0},{3,1},{0,2},{1,3},{6,4},{7,5},{4,6},{5,7},{10,8},{11,9},{8,1... | collective-permute-start | bytes 884744 | tf_op jit(solution)/shard_map/ppermute | solution.py:297
  56.1 15.2 %collective-permute-start.13 = (bf16[96,1536]{1,0:T(8,128)(2,1)S(1)}, bf16[96,1536]{1,0:T(8,128)(2,1)S(1)}, u32[]{:S(2)}, u32[]{:S(2)}) collective-permute-start(bf16[96,1536]{1,0:T(8,128)(2,1)S(1)} %collective-permute-done.2.refs_0_), channel_id=1, source_target_pairs={{3,0},{0,1},{1,2},{2,3},{7,4},{4,5},{5,6},{6,7},{11,8},{8,9},{9,10... | collective-permute-start | bytes 884744 | tf_op jit(solution)/shard_map/ppermute | solution.py:297
  56.5 7.7 %collective-permute-start.3 = (bf16[96,1536]{1,0:T(8,128)(2,1)S(1)}, bf16[96,1536]{1,0:T(8,128)(2,1)S(1)}, u32[]{:S(2)}, u32[]{:S(2)}) collective-permute-start(bf16[96,1536]{1,0:T(8,128)(2,1)S(1)} %collective-permute-done.2.refs_0_), channel_id=1, source_target_pairs={{0,4},{1,5},{2,6},{3,7},{4,0},{5,1},{6,2},{7,3},{8,12},{9,13},{10,... | collective-permute-start | bytes 884744 | tf_op jit(solution)/shard_map/ppermute | solution.py:293
  64.2 44.4 %collective-permute-start.10 = (bf16[96,1536]{1,0:T(8,128)(2,1)S(1)}, bf16[96,1536]{1,0:T(8,128)(2,1)S(1)}, u32[]{:S(2)}, u32[]{:S(2)}) collective-permute-start(bf16[96,1536]{1,0:T(8,128)(2,1)S(1)} %collective-permute-done.3.refs_0_), channel_id=1, source_target_pairs={{3,0},{0,1},{1,2},{2,3},{7,4},{4,5},{5,6},{6,7},{11,8},{8,9},{9,10... | collective-permute-start | bytes 884744 | tf_op jit(solution)/shard_map/ppermute | solution.py:297
  65.9 44.7 %collective-permute-start.8 = (bf16[96,1536]{1,0:T(8,128)(2,1)S(1)}, bf16[96,1536]{1,0:T(8,128)(2,1)S(1)}, u32[]{:S(2)}, u32[]{:S(2)}) collective-permute-start(bf16[96,1536]{1,0:T(8,128)(2,1)S(1)} %collective-permute-done.3.refs_0_), channel_id=1, source_target_pairs={{1,0},{2,1},{3,2},{0,3},{5,4},{6,5},{7,6},{4,7},{9,8},{10,9},{11,1... | collective-permute-start | bytes 884744 | tf_op jit(solution)/shard_map/ppermute | solution.py:297
  66.2 44.4 %collective-permute-start.9 = (bf16[96,1536]{1,0:T(8,128)(2,1)S(1)}, bf16[96,1536]{1,0:T(8,128)(2,1)S(1)}, u32[]{:S(2)}, u32[]{:S(2)}) collective-permute-start(bf16[96,1536]{1,0:T(8,128)(2,1)S(1)} %collective-permute-done.3.refs_0_), channel_id=1, source_target_pairs={{2,0},{3,1},{0,2},{1,3},{6,4},{7,5},{4,6},{5,7},{10,8},{11,9},{8,1... | collective-permute-start | bytes 884744 | tf_op jit(solution)/shard_map/ppermute | solution.py:297
  69.1 27.9 %collective-permute-start.4 = (bf16[96,1536]{1,0:T(8,128)(2,1)S(1)}, bf16[96,1536]{1,0:T(8,128)(2,1)S(1)}, u32[]{:S(2)}, u32[]{:S(2)}) collective-permute-start(bf16[96,1536]{1,0:T(8,128)(2,1)S(1)} %collective-permute-done.3.refs_0_), channel_id=1, source_target_pairs={{0,28},{1,29},{2,30},{3,31},{4,8},{5,9},{6,10},{7,11},{8,4},{9,5},... | collective-permute-start | bytes 884744 | tf_op jit(solution)/shard_map/ppermute | solution.py:293
  97.0 43.7 %collective-permute-start.5 = (bf16[96,1536]{1,0:T(8,128)(2,1)S(1)}, bf16[96,1536]{1,0:T(8,128)(2,1)S(1)}, u32[]{:S(2)}, u32[]{:S(2)}) collective-permute-start(bf16[96,1536]{1,0:T(8,128)(2,1)S(1)} %collective-permute-done.4.refs_0_), channel_id=1, source_target_pairs={{1,0},{2,1},{3,2},{0,3},{5,4},{6,5},{7,6},{4,7},{9,8},{10,9},{11,1... | collective-permute-start | bytes 884744 | tf_op jit(solution)/shard_map/ppermute | solution.py:297
  97.4 43.4 %collective-permute-start.6 = (bf16[96,1536]{1,0:T(8,128)(2,1)S(1)}, bf16[96,1536]{1,0:T(8,128)(2,1)S(1)}, u32[]{:S(2)}, u32[]{:S(2)}) collective-permute-start(bf16[96,1536]{1,0:T(8,128)(2,1)S(1)} %collective-permute-done.4.refs_0_), channel_id=1, source_target_pairs={{2,0},{3,1},{0,2},{1,3},{6,4},{7,5},{4,6},{5,7},{10,8},{11,9},{8,1... | collective-permute-start | bytes 884744 | tf_op jit(solution)/shard_map/ppermute | solution.py:297
  108.6 32.1 %collective-permute-start.7 = (bf16[96,1536]{1,0:T(8,128)(2,1)S(1)}, bf16[96,1536]{1,0:T(8,128)(2,1)S(1)}, u32[]{:S(2)}, u32[]{:S(2)}) collective-permute-start(bf16[96,1536]{1,0:T(8,128)(2,1)S(1)} %collective-permute-done.4.refs_0_), channel_id=1, source_target_pairs={{3,0},{0,1},{1,2},{2,3},{7,4},{4,5},{5,6},{6,7},{11,8},{8,9},{9,10... | collective-permute-start | bytes 884744 | tf_op jit(solution)/shard_map/ppermute | solution.py:297
  182.5 3.9 %copy-start.2 = (f32[1536,1664]{1,0:T(8,128)S(1)}, f32[1536,1664]{1,0:T(8,128)}, u32[]{:S(2)}) copy-start(f32[1536,1664]{1,0:T(8,128)} %all-gather.2.cloned.1.call-done.refs_1_.refs_5_) | copy-start | bytes 30670852
  186.7 0.7 collective-permute-start.20
  187.4 0.7 collective-permute-start.21
  188.1 0.8 collective-permute-start.22
  188.9 6.7 %slice-start.3 = ((s8[10223616]{0:T(1024)(128)(4,1)}), s8[4194304]{0:T(1024)(128)(4,1)S(1)}, s32[]{:S(2)}) async-start(s8[10223616]{0:T(1024)(128)(4,1)} %bitcast.24), calls=%async_computation.4 | async-start | bytes 8388608
  188.9 6.7 %slice-start.4 = ((s8[10223616]{0:T(1024)(128)(4,1)}), s8[4194304]{0:T(1024)(128)(4,1)S(1)}, s32[]{:S(2)}) async-start(s8[10223616]{0:T(1024)(128)(4,1)} %bitcast.24), calls=%async_computation.5 | async-start | bytes 8388608
  189.0 6.7 %slice-start.5 = ((s8[10223616]{0:T(1024)(128)(4,1)}), s8[1835008]{0:T(1024)(128)(4,1)S(1)}, s32[]{:S(2)}) async-start(s8[10223616]{0:T(1024)(128)(4,1)} %bitcast.24), calls=%async_computation.6 | async-start | bytes 3670016
  189.0 6.7 %collective-permute-start.23 = (f32[1,1536]{1,0:T(1,128)S(1)}, f32[1,1536]{1,0:T(1,128)S(1)}, u32[]{:S(2)}, u32[]{:S(2)}) collective-permute-start(f32[1,1536]{1,0:T(1,128)S(1)} %turn3.1.refs_1_), channel_id=1, source_target_pairs={{128,96},{129,97},{130,98},{131,99},{132,100},{133,101},{134,102},... | collective-permute-start | bytes 18440 | tf_op jit(solution)/shard_map/ppermute | solution.py:335
  195.7 0.7 collective-permute-start.24
  196.4 0.7 collective-permute-start.25
  197.1 23.4 %collective-permute-start.26 = (f32[1,1536]{1,0:T(1,128)S(1)}, f32[1,1536]{1,0:T(1,128)S(1)}, u32[]{:S(2)}, u32[]{:S(2)}) collective-permute-start(f32[1,1536]{1,0:T(1,128)S(1)} %turn6.1.refs_1_), channel_id=1, source_target_pairs={{32,0},{33,1},{34,2},{35,3},{36,4},{37,5},{38,6},{39,7},{40,8},{41... | collective-permute-start | bytes 18440 | tf_op jit(solution)/shard_map/ppermute | solution.py:335
  (6 other events, 20.2 us)
Sparse Core Ops, SparseCore 0:
  18.7 123.6 all-gather.1
